TPU v7x, 512 devices: a whole 4x4x16 slice. The times are simulated.
512 devices in a mesh: rep: 32 (over x, y, z_hi), tp: 16 (over z_lo, core).
Axes of the slice: x: 4, y: 4, z: 16 (z_hi: 2, z_lo: 8; z = z_hi * 8 + z_lo), core: 2. Of those that a mesh axis runs over, the one named last changes fastest.
Arguments:
- context: bfloat16 [32, 3, 512, 2560], P('rep', None, 'tp'), may hold values from -6 to 6
- residual: bfloat16 [32, 3, 2560, 512], P('rep', None, 'tp'), may hold values from -6 to 6
- cotangent: bfloat16 [32, 3, 2560, 512], P('rep', None, 'tp'), may hold values from -6 to 6
- norm_gain: bfloat16 [2560], P('tp'), may hold values from 0.099609375 to 1.8984375
- weight: bfloat16 [32, 2560, 2560], P('rep', 'tp'), may hold values from -6 to 6
- momentum: bfloat16 [32, 2560, 2560], P('rep', 'tp'), may hold values from -4 to 4
- round_start: int32 [1], replicated, may hold values from 0 to 31
Outputs:
- weight_out: bfloat16 [32, 2560, 2560], P('rep', 'tp')
- momentum_out: bfloat16 [32, 2560, 2560], P('rep', 'tp')
Inputs may be any that keep to these rules, and one draw needn't show every extreme that they name: Step s of the window averages with the replica whose index differs in bit number (round_start + s) mod log2(32).
All inputs are finite; a program needn't handle non-finite values.
Results may differ from a plain program's by a relative error of at most 0.015.
Values may be sent and summed in bfloat16 or wider, within the bound.
A program may use at most 64 MiB of HBM per device.

v0:
```python
from functools import partial
import jax
import jax.numpy as jnp
from jax import lax
from jax.sharding import PartitionSpec as P

D = 2560
HF = 2560
STEPS = 3
learn_rate = 0.5
beta_decay = 0.9
epsilon = 1e-05


def as_sent(array):
    return jax.tree.map(lambda a: a.astype(jnp.bfloat16) if a.dtype == jnp.float32 else a, array)


def partner(block, axis, distance):
    count = lax.axis_size(axis)
    route = []
    for low in range(count):
        high = low | 1 << distance
        if high != low and high < count:
            route += [(low, high), (high, low)]
    return lax.ppermute(block, axis, route)


def copy_for_each(array, axis):
    copies = jnp.broadcast_to(array, (lax.axis_size(axis), *array.shape))
    return lax.all_to_all(copies, axis, split_axis=0, concat_axis=0, tiled=True)


def taken_together(array, axis):
    everything = copy_for_each(array, axis)
    return jnp.sum(everything, axis=0)


def together(arrays, axis):
    ravelled, at, finished = (jnp.concatenate([a.reshape(-1) for a in arrays]), 0, [])
    running = taken_together(ravelled, axis)
    for a in arrays:
        finished.append(running[at : at + a.size].reshape(a.shape))
        at += a.size
    return tuple(finished)


def mix_pair(own_value, peer_value):
    return ((own_value.astype(jnp.float32) + peer_value.astype(jnp.float32)) * 0.5).astype(
        jnp.bfloat16
    )


def average_peer(weight_now, moment_now, bit_number):
    peer_weight, peer_moment = (
        partner(as_sent(weight_now), "rep", bit_number).astype(weight_now.dtype),
        partner(as_sent(moment_now), "rep", bit_number).astype(moment_now.dtype),
    )
    return (mix_pair(weight_now, peer_weight), mix_pair(moment_now, peer_moment))


def on_device(context, residual, cotangent, norm_gain, weight, momentum, round_start):
    bit_count = lax.axis_size("rep").bit_length() - 1
    out_scale = HF ** (-0.5)
    gain_values = norm_gain.astype(jnp.float32)[:, None]
    gathered_all = lax.all_gather(context, "tp", axis=2, tiled=True)
    branches = [partial(average_peer, bit_number=number) for number in range(bit_count)]
    weight_now = weight[0]
    moment_now = momentum[0]
    for section in range(STEPS):
        gathered = gathered_all[0, section]
        projected = (
            lax.dot_general(
                weight_now, gathered, (((1,), (1,)), ((), ())), preferred_element_type=jnp.float32
            )
            * out_scale
        )
        hidden = residual[0, section].astype(jnp.float32) + projected
        weighted = cotangent[0, section].astype(jnp.float32) * gain_values
        square_sum, cross_sum = together(
            (
                jnp.sum(hidden * hidden, axis=0, keepdims=True),
                jnp.sum(weighted * hidden, axis=0, keepdims=True),
            ),
            "tp",
        )
        inverse = lax.rsqrt(square_sum / D + epsilon)
        cross_mean = cross_sum / D
        grad_hidden = (
            inverse * weighted - hidden * inverse * inverse * inverse * cross_mean
        ).astype(jnp.bfloat16)
        gradient = jnp.dot(grad_hidden, gathered, preferred_element_type=jnp.float32) * out_scale
        bit_pick = (round_start[0] + section) % bit_count
        fresh_moment = (beta_decay * moment_now.astype(jnp.float32) + gradient).astype(jnp.bfloat16)
        fresh_weight = (
            weight_now.astype(jnp.float32) - learn_rate * fresh_moment.astype(jnp.float32)
        ).astype(jnp.bfloat16)
        weight_now, moment_now = lax.switch(bit_pick, branches, fresh_weight, fresh_moment)
    return (weight_now[None], moment_now[None])


def solution(mesh):
    return jax.shard_map(
        on_device,
        mesh=mesh,
        in_specs=(
            P("rep", None, "tp", None),
            P("rep", None, "tp", None),
            P("rep", None, "tp", None),
            P("tp"),
            P("rep", "tp", None),
            P("rep", "tp", None),
            P(),
        ),
        out_specs=(P("rep", "tp", None), P("rep", "tp", None)),
        check_vma=False,
    )
```

profile of v0, /device:TPU:4, one launch (start us, length us, event | category | flops | bytes accessed | tf_op | source)
XLA Modules:
  0.0 436.2 jit_solution(3433902125749589781)
XLA Ops:
  8.6 121.7 %all-gather.2.cloned.1.call-done = bf16[1,3,512,2560]{3,2,1,0:T(8,128)(2,1)} async-done(((bf16[1,3,32,2560]{3,2,1,0:T(8,128)(2,1)}), bf16[1,3,512,2560]{3,2,1,0:T(8,128)(2,1)}) %all-gather.2.cloned.1.call-update) | async-done | bytes 7864336 | tf_op jit(solution)/shard_map/all_gather | solution.py:66
  130.3 3.0 multiply_reduce_fusion.2
  134.0 5.8 %all-to-all-start = ((f32[16,1,1024]{2,1,0:T(1,128)}), f32[16,1,1024]{2,1,0:T(1,128)S(1)}, u32[]{:S(2)}, u32[]{:S(2)}) async-start(f32[16,1,1024]{2,1,0:T(1,128)} %broadcast_in_dim.42), calls=%async_computation | async-start | bytes 131072 | tf_op jit(solution)/shard_map/all_to_all | solution.py:31
  140.4 10.3 %all-to-all-done = f32[16,1,1024]{2,1,0:T(1,128)S(1)} async-done(((f32[16,1,1024]{2,1,0:T(1,128)}), f32[16,1,1024]{2,1,0:T(1,128)S(1)}, u32[]{:S(2)}, u32[]{:S(2)}) %all-to-all-start) | async-done | bytes 65568 | tf_op jit(solution)/shard_map/all_to_all | solution.py:31
  150.8 2.5 subtract_convert_fusion.2
  153.3 40.9 %conditional.3 = (bf16[160,2560]{1,0:T(8,128)(2,1)S(1)}, f32[160,2560]{1,0:T(8,128)}, f32[160,2560]{1,0:T(8,128)S(1)}) conditional(s32[]{:T(128)} %clamp.11, (bf16[160,2560]{1,0:T(8,128)(2,1)S(1)}, bf16[160,2560]{1,0:T(8,128)(2,1)S(1)}) %subtract_convert_fusion.2, (bf16[160,2560]{1,0:T(8,128)(2,1)S(1)}, ...), branch_computations={%region_3.4_spmd, %region_4.5_spmd, %region_5.6_spmd, %region_6.7_... | conditional | flops 4915200 | bytes 13926504 | solution.py:98
  153.4 2.2 collective-permute-start.18
  155.6 5.1 %collective-permute-start.19 = (bf16[160,2560]{1,0:T(8,128)(2,1)S(1)}, bf16[160,2560]{1,0:T(8,128)(2,1)S(1)}, u32[]{:S(2)}, u32[]{:S(2)}) collective-permute-start(bf16[160,2560]{1,0:T(8,128)(2,1)S(1)} %get-tuple-element.75), channel_id=1, source_target_pairs={{0,256},{256,0},{16,272},{272,16},{32,288},{288,32},{48,304},{304,... | collective-permute-start | bytes 2457608 | tf_op jit(solution)/shard_map/cond/branch_4_fun/ppermute | solution.py:26
  160.7 17.2 %collective-permute-done.18 = bf16[160,2560]{1,0:T(8,128)(2,1)S(1)} collective-permute-done((bf16[160,2560]{1,0:T(8,128)(2,1)S(1)}, bf16[160,2560]{1,0:T(8,128)(2,1)S(1)}, u32[]{:S(2)}, u32[]{:S(2)}) %collective-permute-start.18) | collective-permute-done | bytes 819232 | tf_op jit(solution)/shard_map/cond/branch_4_fun/ppermute | solution.py:26
  177.9 1.5 fusion.73
  179.4 14.6 %collective-permute-done.19 = bf16[160,2560]{1,0:T(8,128)(2,1)S(1)} collective-permute-done((bf16[160,2560]{1,0:T(8,128)(2,1)S(1)}, bf16[160,2560]{1,0:T(8,128)(2,1)S(1)}, u32[]{:S(2)}, u32[]{:S(2)}) %collective-permute-start.19) | collective-permute-done | bytes 819232 | tf_op jit(solution)/shard_map/cond/branch_4_fun/ppermute | solution.py:26
  194.2 2.8 multiply_reduce_fusion.1
  197.7 3.8 all-to-all-start.1
  201.5 10.9 %all-to-all-done.1 = f32[16,1,1024]{2,1,0:T(1,128)S(1)} async-done(((f32[16,1,1024]{2,1,0:T(1,128)}), f32[16,1,1024]{2,1,0:T(1,128)S(1)}, u32[]{:S(2)}, u32[]{:S(2)}) %all-to-all-start.1) | async-done | bytes 65568 | tf_op jit(solution)/shard_map/all_to_all | solution.py:31
  212.5 3.0 subtract_convert_fusion.1
  215.6 140.3 %conditional.4 = (bf16[160,2560]{1,0:T(8,128)(2,1)S(1)}, f32[160,2560]{1,0:T(8,128)}, f32[160,2560]{1,0:T(8,128)S(1)}) conditional(s32[]{:T(128)} %clamp.10, (bf16[160,2560]{1,0:T(8,128)(2,1)S(1)}, bf16[160,2560]{1,0:T(8,128)(2,1)S(1)}) %subtract_convert_fusion.1, (bf16[160,2560]{1,0:T(8,128)(2,1)S(1)}, ...), branch_computations={%region_11.12_spmd, %region_12.13_spmd, %region_13.14_spmd, %regio... | conditional | flops 4915200 | bytes 13926504 | solution.py:98
  215.6 8.8 %collective-permute-start.20 = (bf16[160,2560]{1,0:T(8,128)(2,1)S(1)}, bf16[160,2560]{1,0:T(8,128)(2,1)S(1)}, u32[]{:S(2)}, u32[]{:S(2)}) collective-permute-start(bf16[160,2560]{1,0:T(8,128)(2,1)S(1)} %get-tuple-element.76), channel_id=1, source_target_pairs={{0,16},{16,0},{32,48},{48,32},{64,80},{80,64},{96,112},{112,96},{1... | collective-permute-start | bytes 2457608 | tf_op jit(solution)/shard_map/cond/branch_0_fun/ppermute | solution.py:26
  224.4 5.7 %collective-permute-start.21 = (bf16[160,2560]{1,0:T(8,128)(2,1)S(1)}, bf16[160,2560]{1,0:T(8,128)(2,1)S(1)}, u32[]{:S(2)}, u32[]{:S(2)}) collective-permute-start(bf16[160,2560]{1,0:T(8,128)(2,1)S(1)} %get-tuple-element.77), channel_id=1, source_target_pairs={{0,16},{16,0},{32,48},{48,32},{64,80},{80,64},{96,112},{112,96},{1... | collective-permute-start | bytes 2457608 | tf_op jit(solution)/shard_map/cond/branch_0_fun/ppermute | solution.py:26
  230.2 104.7 %collective-permute-done.20 = bf16[160,2560]{1,0:T(8,128)(2,1)S(1)} collective-permute-done((bf16[160,2560]{1,0:T(8,128)(2,1)S(1)}, bf16[160,2560]{1,0:T(8,128)(2,1)S(1)}, u32[]{:S(2)}, u32[]{:S(2)}) %collective-permute-start.20) | collective-permute-done | bytes 819232 | tf_op jit(solution)/shard_map/cond/branch_0_fun/ppermute | solution.py:26
  334.9 1.5 fusion.74
  336.4 19.1 %collective-permute-done.21 = bf16[160,2560]{1,0:T(8,128)(2,1)S(1)} collective-permute-done((bf16[160,2560]{1,0:T(8,128)(2,1)S(1)}, bf16[160,2560]{1,0:T(8,128)(2,1)S(1)}, u32[]{:S(2)}, u32[]{:S(2)}) %collective-permute-start.21) | collective-permute-done | bytes 819232 | tf_op jit(solution)/shard_map/cond/branch_0_fun/ppermute | solution.py:26
  355.9 2.8 multiply_reduce_fusion
  359.3 15.7 %all-to-all-start.2 = ((f32[16,1,1024]{2,1,0:T(1,128)}), f32[16,1,1024]{2,1,0:T(1,128)S(1)}, u32[]{:S(2)}, u32[]{:S(2)}) async-start(f32[16,1,1024]{2,1,0:T(1,128)} %broadcast_in_dim.44), calls=%async_computation.2 | async-start | bytes 131072 | tf_op jit(solution)/shard_map/all_to_all | solution.py:31
  375.0 10.9 %all-to-all-done.2 = f32[16,1,1024]{2,1,0:T(1,128)S(1)} async-done(((f32[16,1,1024]{2,1,0:T(1,128)}), f32[16,1,1024]{2,1,0:T(1,128)S(1)}, u32[]{:S(2)}, u32[]{:S(2)}) %all-to-all-start.2) | async-done | bytes 65568 | tf_op jit(solution)/shard_map/all_to_all | solution.py:31
  386.0 3.0 subtract_convert_fusion
  389.1 40.3 %conditional.5 = (bf16[1,160,2560]{2,1,0:T(8,128)(2,1)}, bf16[1,160,2560]{2,1,0:T(8,128)(2,1)}) conditional(s32[]{:T(128)} %clamp.9, (bf16[160,2560]{1,0:T(8,128)(2,1)S(1)}, bf16[160,2560]{1,0:T(8,128)(2,1)S(1)}) %subtract_convert_fusion, (bf16[160,2560]{1,0:T(8,128)(2,1)S(1)}, ...), branch_computations={%region_19.20_spmd, %region_20.21_spmd, %region_21.22_spmd, %regio... | conditional | flops 4096000 | bytes 11468896 | solution.py:98
  389.1 3.3 collective-permute-start.2
  392.4 2.5 collective-permute-start.3
  395.0 17.1 %collective-permute-done.2 = bf16[160,2560]{1,0:T(8,128)(2,1)S(1)} collective-permute-done((bf16[160,2560]{1,0:T(8,128)(2,1)S(1)}, bf16[160,2560]{1,0:T(8,128)(2,1)S(1)}, u32[]{:S(2)}, u32[]{:S(2)}) %collective-permute-start.2) | collective-permute-done | bytes 819232 | tf_op jit(solution)/shard_map/cond/branch_1_fun/ppermute | solution.py:26
  412.1 1.1 fusion.12
  413.3 15.0 %collective-permute-done.3 = bf16[160,2560]{1,0:T(8,128)(2,1)S(1)} collective-permute-done((bf16[160,2560]{1,0:T(8,128)(2,1)S(1)}, bf16[160,2560]{1,0:T(8,128)(2,1)S(1)}, u32[]{:S(2)}, u32[]{:S(2)}) %collective-permute-start.3) | collective-permute-done | bytes 819232 | tf_op jit(solution)/shard_map/cond/branch_1_fun/ppermute | solution.py:26
  428.2 1.1 fusion.13
  (23 shorter events, 4.0 us)
Async XLA Ops:
  7.2 123.1 %all-gather.2.cloned.1.call-start = ((), (), s32[]{:S(2)}) async-start(), calls=%async_computation.3 | async-start | bytes 8355840 | tf_op jit(solution)/shard_map/all_gather | solution.py:66
  8.6 142.2 %copy-start = (bf16[1,3,160,512]{3,2,1,0:T(8,128)(2,1)S(1)}, bf16[1,3,160,512]{3,2,1,0:T(8,128)(2,1)}, u32[]{:S(2)}) copy-start(bf16[1,3,160,512]{3,2,1,0:T(8,128)(2,1)} %param.24) | copy-start | bytes 1474564
  8.6 142.2 %copy-start.1 = (bf16[1,160,2560]{2,1,0:T(8,128)(2,1)S(1)}, bf16[1,160,2560]{2,1,0:T(8,128)(2,1)}, u32[]{:S(2)}) copy-start(bf16[1,160,2560]{2,1,0:T(8,128)(2,1)} %param.26) | copy-start | bytes 2457604
  8.6 142.2 %copy-start.2 = (bf16[1,160,2560]{2,1,0:T(8,128)(2,1)S(1)}, bf16[1,160,2560]{2,1,0:T(8,128)(2,1)}, u32[]{:S(2)}) copy-start(bf16[1,160,2560]{2,1,0:T(8,128)(2,1)} %param.27) | copy-start | bytes 2457604
  134.0 16.7 %all-to-all-start = ((f32[16,1,1024]{2,1,0:T(1,128)}), f32[16,1,1024]{2,1,0:T(1,128)S(1)}, u32[]{:S(2)}, u32[]{:S(2)}) async-start(f32[16,1,1024]{2,1,0:T(1,128)} %broadcast_in_dim.42), calls=%async_computation | async-start | bytes 131072 | tf_op jit(solution)/shard_map/all_to_all | solution.py:31
  153.4 24.5 %collective-permute-start.18 = (bf16[160,2560]{1,0:T(8,128)(2,1)S(1)}, bf16[160,2560]{1,0:T(8,128)(2,1)S(1)}, u32[]{:S(2)}, u32[]{:S(2)}) collective-permute-start(bf16[160,2560]{1,0:T(8,128)(2,1)S(1)} %get-tuple-element.74), channel_id=1, source_target_pairs={{0,256},{256,0},{16,272},{272,16},{32,288},{288,32},{48,304},{304,... | collective-permute-start | bytes 2457608 | tf_op jit(solution)/shard_map/cond/branch_4_fun/ppermute | solution.py:26
  155.6 38.4 %collective-permute-start.19 = (bf16[160,2560]{1,0:T(8,128)(2,1)S(1)}, bf16[160,2560]{1,0:T(8,128)(2,1)S(1)}, u32[]{:S(2)}, u32[]{:S(2)}) collective-permute-start(bf16[160,2560]{1,0:T(8,128)(2,1)S(1)} %get-tuple-element.75), channel_id=1, source_target_pairs={{0,256},{256,0},{16,272},{272,16},{32,288},{288,32},{48,304},{304,... | collective-permute-start | bytes 2457608 | tf_op jit(solution)/shard_map/cond/branch_4_fun/ppermute | solution.py:26
  197.7 14.8 %all-to-all-start.1 = ((f32[16,1,1024]{2,1,0:T(1,128)}), f32[16,1,1024]{2,1,0:T(1,128)S(1)}, u32[]{:S(2)}, u32[]{:S(2)}) async-start(f32[16,1,1024]{2,1,0:T(1,128)} %broadcast_in_dim.43), calls=%async_computation.1 | async-start | bytes 131072 | tf_op jit(solution)/shard_map/all_to_all | solution.py:31
  215.6 119.3 %collective-permute-start.20 = (bf16[160,2560]{1,0:T(8,128)(2,1)S(1)}, bf16[160,2560]{1,0:T(8,128)(2,1)S(1)}, u32[]{:S(2)}, u32[]{:S(2)}) collective-permute-start(bf16[160,2560]{1,0:T(8,128)(2,1)S(1)} %get-tuple-element.76), channel_id=1, source_target_pairs={{0,16},{16,0},{32,48},{48,32},{64,80},{80,64},{96,112},{112,96},{1... | collective-permute-start | bytes 2457608 | tf_op jit(solution)/shard_map/cond/branch_0_fun/ppermute | solution.py:26
  224.4 131.0 %collective-permute-start.21 = (bf16[160,2560]{1,0:T(8,128)(2,1)S(1)}, bf16[160,2560]{1,0:T(8,128)(2,1)S(1)}, u32[]{:S(2)}, u32[]{:S(2)}) collective-permute-start(bf16[160,2560]{1,0:T(8,128)(2,1)S(1)} %get-tuple-element.77), channel_id=1, source_target_pairs={{0,16},{16,0},{32,48},{48,32},{64,80},{80,64},{96,112},{112,96},{1... | collective-permute-start | bytes 2457608 | tf_op jit(solution)/shard_map/cond/branch_0_fun/ppermute | solution.py:26
  359.3 26.6 %all-to-all-start.2 = ((f32[16,1,1024]{2,1,0:T(1,128)}), f32[16,1,1024]{2,1,0:T(1,128)S(1)}, u32[]{:S(2)}, u32[]{:S(2)}) async-start(f32[16,1,1024]{2,1,0:T(1,128)} %broadcast_in_dim.44), calls=%async_computation.2 | async-start | bytes 131072 | tf_op jit(solution)/shard_map/all_to_all | solution.py:31
  389.1 23.0 %collective-permute-start.2 = (bf16[160,2560]{1,0:T(8,128)(2,1)S(1)}, bf16[160,2560]{1,0:T(8,128)(2,1)S(1)}, u32[]{:S(2)}, u32[]{:S(2)}) collective-permute-start(bf16[160,2560]{1,0:T(8,128)(2,1)S(1)} %get-tuple-element.88), channel_id=1, source_target_pairs={{0,32},{32,0},{16,48},{48,16},{64,96},{96,64},{80,112},{112,80},{1... | collective-permute-start | bytes 2457608 | tf_op jit(solution)/shard_map/cond/branch_1_fun/ppermute | solution.py:26
  392.4 35.8 %collective-permute-start.3 = (bf16[160,2560]{1,0:T(8,128)(2,1)S(1)}, bf16[160,2560]{1,0:T(8,128)(2,1)S(1)}, u32[]{:S(2)}, u32[]{:S(2)}) collective-permute-start(bf16[160,2560]{1,0:T(8,128)(2,1)S(1)} %get-tuple-element.89), channel_id=1, source_target_pairs={{0,32},{32,0},{16,48},{48,16},{64,96},{96,64},{80,112},{112,80},{1... | collective-permute-start | bytes 2457608 | tf_op jit(solution)/shard_map/cond/branch_1_fun/ppermute | solution.py:26
Sparse Core Ops, SparseCore 0:
  10.1 120.1 all-gather.1
where the time goes:
time: 437 us; the launch traced here: 436 us
  waiting for transfers between devices  342 us (78%)
  starting transfers between devices  53 us (12%)
  matrix products  17.2 us (4%)
  between operations  14.9 us (3%)
  other arithmetic  6.56 us (2%)
    ppermute x6, waiting for transfers between devices, partner(): return lax.ppermute(block, axis, route)  188 us
    all_gather x1, waiting for transfers between devices, on_device(): gathered_all = lax.all_gather(context, 'tp', axis=2, tiled=True)  122 us
    all_to_all x3, waiting for transfers between devices, copy_for_each(): return lax.all_to_all(copies, axis, split_axis=0, concat_axis=0, tiled=True)  32.1 us
    ppermute x6, starting transfers between devices, partner(): return lax.ppermute(block, axis, route)  27.7 us
    all_to_all x3, starting transfers between devices, copy_for_each(): return lax.all_to_all(copies, axis, split_axis=0, concat_axis=0, tiled=True)  25.3 us
  transfers between devices with their start and end apart: 10, of which 10 were waited for; matrix products, arithmetic and copies ran while one was open for 1% of the time, Pallas kernels for 0%

commit v1 on v0

--- a/solution.py
+++ b/solution.py
@@ -63,7 +63,9 @@
     bit_count = lax.axis_size("rep").bit_length() - 1
     out_scale = HF ** (-0.5)
     gain_values = norm_gain.astype(jnp.float32)[:, None]
-    gathered_all = lax.all_gather(context, "tp", axis=2, tiled=True)
+    gathered_all = jnp.concatenate(
+        lax.all_to_all(jnp.stack([context] * lax.axis_size("tp")), "tp", 0, 0), axis=2
+    )
     branches = [partial(average_peer, bit_number=number) for number in range(bit_count)]
     weight_now = weight[0]
     moment_now = momentum[0]

time: 437 us -> 665 us (1.52)
  the two profiles are of different devices: /device:TPU:4 before, /device:TPU:26 now
where the time goes in v1:
time: 665 us; the launch traced here: 664 us
  waiting for transfers between devices  505 us (76%)
  starting transfers between devices  122 us (18%)
  matrix products  17 us (3%)
  local copies, waits for them, and re-layouts  13.9 us (2%)
    all_to_all x1, waiting for transfers between devices, on_device(): lax.all_to_all(jnp.stack([context] * lax.axis_size('tp')), 'tp', 0, 0)  282 us
    ppermute x6, waiting for transfers between devices, partner(): return lax.ppermute(block, axis, route)  191 us
    all_to_all x3, starting transfers between devices, copy_for_each(): return lax.all_to_all(copies, axis, split_axis=0, concat_axis=0, tiled=True)  81.3 us
    all_to_all x3, waiting for transfers between devices, copy_for_each(): return lax.all_to_all(copies, axis, split_axis=0, concat_axis=0, tiled=True)  32.1 us
    ppermute x6, starting transfers between devices, partner(): return lax.ppermute(block, axis, route)  27.7 us
  transfers between devices with their start and end apart: 10, of which 10 were waited for; matrix products, arithmetic and copies ran while one was open for 0% of the time, Pallas kernels for 0%

profile of v1, /device:TPU:26, one launch (start us, length us, event | category | flops | bytes accessed | tf_op | source)
XLA Modules:
  0.0 664.2 jit_solution(9539358707952534449)
XLA Ops:
  0.6 5.1 stack.2
  5.7 12.8 %all-to-all-start = ((bf16[16,1,3,32,2560]{4,3,2,1,0:T(8,128)(2,1)}), bf16[16,1,3,32,2560]{4,3,2,1,0:T(8,128)(2,1)}, u32[]{:S(2)}, u32[]{:S(2)}) async-start(bf16[16,1,3,32,2560]{4,3,2,1,0:T(8,128)(2,1)} %stack.2), calls=%async_computation | async-start | bytes 15728640 | tf_op jit(solution)/shard_map/all_to_all | solution.py:67
  18.6 281.6 %all-to-all-done = bf16[16,1,3,32,2560]{4,3,2,1,0:T(8,128)(2,1)} async-done(((bf16[16,1,3,32,2560]{4,3,2,1,0:T(8,128)(2,1)}), bf16[16,1,3,32,2560]{4,3,2,1,0:T(8,128)(2,1)}, u32[]{:S(2)}, u32[]{:S(2)}) %all-to-all-start) | async-done | bytes 7864352 | tf_op jit(solution)/shard_map/all_to_all | solution.py:67
  300.1 3.7 copy.21
  303.9 3.0 copy-done
  306.9 2.0 multiply_reduce_fusion.2
  309.6 64.5 %all-to-all-start.1 = ((f32[16,1,1024]{2,1,0:T(1,128)}), f32[16,1,1024]{2,1,0:T(1,128)S(1)}, u32[]{:S(2)}, u32[]{:S(2)}) async-start(f32[16,1,1024]{2,1,0:T(1,128)} %broadcast_in_dim.42), calls=%async_computation.1 | async-start | bytes 131072 | tf_op jit(solution)/shard_map/all_to_all | solution.py:31
  374.8 10.3 %all-to-all-done.1 = f32[16,1,1024]{2,1,0:T(1,128)S(1)} async-done(((f32[16,1,1024]{2,1,0:T(1,128)}), f32[16,1,1024]{2,1,0:T(1,128)S(1)}, u32[]{:S(2)}, u32[]{:S(2)}) %all-to-all-start.1) | async-done | bytes 65568 | tf_op jit(solution)/shard_map/all_to_all | solution.py:31
  385.1 2.7 subtract_convert_fusion.2
  387.9 40.9 %conditional.3 = (bf16[160,2560]{1,0:T(8,128)(2,1)S(1)}, f32[160,2560]{1,0:T(8,128)}, f32[160,2560]{1,0:T(8,128)S(1)}) conditional(s32[]{:T(128)} %clamp.11, (bf16[160,2560]{1,0:T(8,128)(2,1)S(1)}, bf16[160,2560]{1,0:T(8,128)(2,1)S(1)}) %subtract_convert_fusion.2, (bf16[160,2560]{1,0:T(8,128)(2,1)S(1)}, ...), branch_computations={%region_3.4_spmd, %region_4.5_spmd, %region_5.6_spmd, %region_6.7_... | conditional | flops 4915200 | bytes 13926504 | solution.py:100
  387.9 4.0 collective-permute-start.18
  392.0 3.3 collective-permute-start.19
  395.3 17.1 %collective-permute-done.18 = bf16[160,2560]{1,0:T(8,128)(2,1)S(1)} collective-permute-done((bf16[160,2560]{1,0:T(8,128)(2,1)S(1)}, bf16[160,2560]{1,0:T(8,128)(2,1)S(1)}, u32[]{:S(2)}, u32[]{:S(2)}) %collective-permute-start.18) | collective-permute-done | bytes 819232 | tf_op jit(solution)/shard_map/cond/branch_4_fun/ppermute | solution.py:26
  413.9 14.6 %collective-permute-done.19 = bf16[160,2560]{1,0:T(8,128)(2,1)S(1)} collective-permute-done((bf16[160,2560]{1,0:T(8,128)(2,1)S(1)}, bf16[160,2560]{1,0:T(8,128)(2,1)S(1)}, u32[]{:S(2)}, u32[]{:S(2)}) %collective-permute-start.19) | collective-permute-done | bytes 819232 | tf_op jit(solution)/shard_map/cond/branch_4_fun/ppermute | solution.py:26
  428.7 2.9 multiply_reduce_fusion.1
  432.3 3.8 all-to-all-start.2
  436.2 10.9 %all-to-all-done.2 = f32[16,1,1024]{2,1,0:T(1,128)S(1)} async-done(((f32[16,1,1024]{2,1,0:T(1,128)}), f32[16,1,1024]{2,1,0:T(1,128)S(1)}, u32[]{:S(2)}, u32[]{:S(2)}) %all-to-all-start.2) | async-done | bytes 65568 | tf_op jit(solution)/shard_map/all_to_all | solution.py:31
  447.1 3.1 subtract_convert_fusion.1
  450.2 142.7 %conditional.4 = (bf16[160,2560]{1,0:T(8,128)(2,1)S(1)}, f32[160,2560]{1,0:T(8,128)S(1)}, f32[160,2560]{1,0:T(8,128)S(1)}) conditional(s32[]{:T(128)} %clamp.10, (bf16[160,2560]{1,0:T(8,128)(2,1)S(1)}, bf16[160,2560]{1,0:T(8,128)(2,1)S(1)}) %subtract_convert_fusion.1, (bf16[160,2560]{1,0:T(8,128)(2,1)S(1)}, ...), branch_computations={%region_11.12_spmd, %region_12.13_spmd, %region_13.14_spmd, %regio... | conditional | flops 4915200 | bytes 13926504 | solution.py:100
  450.2 8.2 %collective-permute-start.20 = (bf16[160,2560]{1,0:T(8,128)(2,1)S(1)}, bf16[160,2560]{1,0:T(8,128)(2,1)S(1)}, u32[]{:S(2)}, u32[]{:S(2)}) collective-permute-start(bf16[160,2560]{1,0:T(8,128)(2,1)S(1)} %get-tuple-element.76), channel_id=1, source_target_pairs={{0,16},{16,0},{32,48},{48,32},{64,80},{80,64},{96,112},{112,96},{1... | collective-permute-start | bytes 2457608 | tf_op jit(solution)/shard_map/cond/branch_0_fun/ppermute | solution.py:26
  458.5 6.3 collective-permute-start.21
  464.8 105.8 %collective-permute-done.20 = bf16[160,2560]{1,0:T(8,128)(2,1)S(1)} collective-permute-done((bf16[160,2560]{1,0:T(8,128)(2,1)S(1)}, bf16[160,2560]{1,0:T(8,128)(2,1)S(1)}, u32[]{:S(2)}, u32[]{:S(2)}) %collective-permute-start.20) | collective-permute-done | bytes 819232 | tf_op jit(solution)/shard_map/cond/branch_0_fun/ppermute | solution.py:26
  570.9 21.6 %collective-permute-done.21 = bf16[160,2560]{1,0:T(8,128)(2,1)S(1)} collective-permute-done((bf16[160,2560]{1,0:T(8,128)(2,1)S(1)}, bf16[160,2560]{1,0:T(8,128)(2,1)S(1)}, u32[]{:S(2)}, u32[]{:S(2)}) %collective-permute-start.21) | collective-permute-done | bytes 819232 | tf_op jit(solution)/shard_map/cond/branch_0_fun/ppermute | solution.py:26
  592.9 3.6 multiply_reduce_fusion
  597.2 13.0 %all-to-all-start.3 = ((f32[16,1,1024]{2,1,0:T(1,128)}), f32[16,1,1024]{2,1,0:T(1,128)S(1)}, u32[]{:S(2)}, u32[]{:S(2)}) async-start(f32[16,1,1024]{2,1,0:T(1,128)} %broadcast_in_dim.44), calls=%async_computation.3 | async-start | bytes 131072 | tf_op jit(solution)/shard_map/all_to_all | solution.py:31
  610.2 10.9 %all-to-all-done.3 = f32[16,1,1024]{2,1,0:T(1,128)S(1)} async-done(((f32[16,1,1024]{2,1,0:T(1,128)}), f32[16,1,1024]{2,1,0:T(1,128)S(1)}, u32[]{:S(2)}, u32[]{:S(2)}) %all-to-all-start.3) | async-done | bytes 65568 | tf_op jit(solution)/shard_map/all_to_all | solution.py:31
  621.2 2.7 subtract_convert_fusion
  624.0 40.3 %conditional.5 = (bf16[1,160,2560]{2,1,0:T(8,128)(2,1)}, bf16[1,160,2560]{2,1,0:T(8,128)(2,1)}) conditional(s32[]{:T(128)} %clamp.9, (bf16[160,2560]{1,0:T(8,128)(2,1)S(1)}, bf16[160,2560]{1,0:T(8,128)(2,1)S(1)}) %subtract_convert_fusion, (bf16[160,2560]{1,0:T(8,128)(2,1)S(1)}, ...), branch_computations={%region_19.20_spmd, %region_20.21_spmd, %region_21.22_spmd, %regio... | conditional | flops 4096000 | bytes 11468896 | solution.py:100
  624.0 2.7 collective-permute-start.2
  626.6 3.2 collective-permute-start.3
  629.8 17.1 %collective-permute-done.2 = bf16[160,2560]{1,0:T(8,128)(2,1)S(1)} collective-permute-done((bf16[160,2560]{1,0:T(8,128)(2,1)S(1)}, bf16[160,2560]{1,0:T(8,128)(2,1)S(1)}, u32[]{:S(2)}, u32[]{:S(2)}) %collective-permute-start.2) | collective-permute-done | bytes 819232 | tf_op jit(solution)/shard_map/cond/branch_1_fun/ppermute | solution.py:26
  648.1 15.0 %collective-permute-done.3 = bf16[160,2560]{1,0:T(8,128)(2,1)S(1)} collective-permute-done((bf16[160,2560]{1,0:T(8,128)(2,1)S(1)}, bf16[160,2560]{1,0:T(8,128)(2,1)S(1)}, u32[]{:S(2)}, u32[]{:S(2)}) %collective-permute-start.3) | collective-permute-done | bytes 819232 | tf_op jit(solution)/shard_map/cond/branch_1_fun/ppermute | solution.py:26
  (26 shorter events, 6.7 us)
Async XLA Ops:
  5.7 12.8 %copy-start.3 = (bf16[160]{0:T(256)(128)(2,1)S(1)}, bf16[160]{0:T(256)(128)(2,1)}, u32[]{:S(2)}) copy-start(bf16[160]{0:T(256)(128)(2,1)} %param.25) | copy-start | bytes 964
  5.7 294.4 %all-to-all-start = ((bf16[16,1,3,32,2560]{4,3,2,1,0:T(8,128)(2,1)}), bf16[16,1,3,32,2560]{4,3,2,1,0:T(8,128)(2,1)}, u32[]{:S(2)}, u32[]{:S(2)}) async-start(bf16[16,1,3,32,2560]{4,3,2,1,0:T(8,128)(2,1)} %stack.2), calls=%async_computation | async-start | bytes 15728640 | tf_op jit(solution)/shard_map/all_to_all | solution.py:67
  18.5 288.4 %copy-start.1 = (bf16[1,3,160,512]{3,2,1,0:T(8,128)(2,1)S(1)}, bf16[1,3,160,512]{3,2,1,0:T(8,128)(2,1)}, u32[]{:S(2)}) copy-start(bf16[1,3,160,512]{3,2,1,0:T(8,128)(2,1)} %param.24) | copy-start | bytes 1474564
  18.5 288.4 %copy-start.2 = (bf16[1,160,2560]{2,1,0:T(8,128)(2,1)S(1)}, bf16[1,160,2560]{2,1,0:T(8,128)(2,1)}, u32[]{:S(2)}) copy-start(bf16[1,160,2560]{2,1,0:T(8,128)(2,1)} %param.26) | copy-start | bytes 2457604
  303.9 3.1 copy-start
  309.6 75.5 %all-to-all-start.1 = ((f32[16,1,1024]{2,1,0:T(1,128)}), f32[16,1,1024]{2,1,0:T(1,128)S(1)}, u32[]{:S(2)}, u32[]{:S(2)}) async-start(f32[16,1,1024]{2,1,0:T(1,128)} %broadcast_in_dim.42), calls=%async_computation.1 | async-start | bytes 131072 | tf_op jit(solution)/shard_map/all_to_all | solution.py:31
  387.9 24.5 %collective-permute-start.18 = (bf16[160,2560]{1,0:T(8,128)(2,1)S(1)}, bf16[160,2560]{1,0:T(8,128)(2,1)S(1)}, u32[]{:S(2)}, u32[]{:S(2)}) collective-permute-start(bf16[160,2560]{1,0:T(8,128)(2,1)S(1)} %get-tuple-element.74), channel_id=1, source_target_pairs={{0,256},{256,0},{16,272},{272,16},{32,288},{288,32},{48,304},{304,... | collective-permute-start | bytes 2457608 | tf_op jit(solution)/shard_map/cond/branch_4_fun/ppermute | solution.py:26
  392.0 36.6 %collective-permute-start.19 = (bf16[160,2560]{1,0:T(8,128)(2,1)S(1)}, bf16[160,2560]{1,0:T(8,128)(2,1)S(1)}, u32[]{:S(2)}, u32[]{:S(2)}) collective-permute-start(bf16[160,2560]{1,0:T(8,128)(2,1)S(1)} %get-tuple-element.75), channel_id=1, source_target_pairs={{0,256},{256,0},{16,272},{272,16},{32,288},{288,32},{48,304},{304,... | collective-permute-start | bytes 2457608 | tf_op jit(solution)/shard_map/cond/branch_4_fun/ppermute | solution.py:26
  432.3 14.8 %all-to-all-start.2 = ((f32[16,1,1024]{2,1,0:T(1,128)}), f32[16,1,1024]{2,1,0:T(1,128)S(1)}, u32[]{:S(2)}, u32[]{:S(2)}) async-start(f32[16,1,1024]{2,1,0:T(1,128)} %broadcast_in_dim.43), calls=%async_computation.2 | async-start | bytes 131072 | tf_op jit(solution)/shard_map/all_to_all | solution.py:31
  450.2 120.4 %collective-permute-start.20 = (bf16[160,2560]{1,0:T(8,128)(2,1)S(1)}, bf16[160,2560]{1,0:T(8,128)(2,1)S(1)}, u32[]{:S(2)}, u32[]{:S(2)}) collective-permute-start(bf16[160,2560]{1,0:T(8,128)(2,1)S(1)} %get-tuple-element.76), channel_id=1, source_target_pairs={{0,16},{16,0},{32,48},{48,32},{64,80},{80,64},{96,112},{112,96},{1... | collective-permute-start | bytes 2457608 | tf_op jit(solution)/shard_map/cond/branch_0_fun/ppermute | solution.py:26
  458.5 134.1 %collective-permute-start.21 = (bf16[160,2560]{1,0:T(8,128)(2,1)S(1)}, bf16[160,2560]{1,0:T(8,128)(2,1)S(1)}, u32[]{:S(2)}, u32[]{:S(2)}) collective-permute-start(bf16[160,2560]{1,0:T(8,128)(2,1)S(1)} %get-tuple-element.77), channel_id=1, source_target_pairs={{0,16},{16,0},{32,48},{48,32},{64,80},{80,64},{96,112},{112,96},{1... | collective-permute-start | bytes 2457608 | tf_op jit(solution)/shard_map/cond/branch_0_fun/ppermute | solution.py:26
  597.2 23.9 %all-to-all-start.3 = ((f32[16,1,1024]{2,1,0:T(1,128)}), f32[16,1,1024]{2,1,0:T(1,128)S(1)}, u32[]{:S(2)}, u32[]{:S(2)}) async-start(f32[16,1,1024]{2,1,0:T(1,128)} %broadcast_in_dim.44), calls=%async_computation.3 | async-start | bytes 131072 | tf_op jit(solution)/shard_map/all_to_all | solution.py:31
  624.0 23.0 %collective-permute-start.2 = (bf16[160,2560]{1,0:T(8,128)(2,1)S(1)}, bf16[160,2560]{1,0:T(8,128)(2,1)S(1)}, u32[]{:S(2)}, u32[]{:S(2)}) collective-permute-start(bf16[160,2560]{1,0:T(8,128)(2,1)S(1)} %get-tuple-element.88), channel_id=1, source_target_pairs={{0,32},{32,0},{16,48},{48,16},{64,96},{96,64},{80,112},{112,80},{1... | collective-permute-start | bytes 2457608 | tf_op jit(solution)/shard_map/cond/branch_1_fun/ppermute | solution.py:26
  626.6 36.5 %collective-permute-start.3 = (bf16[160,2560]{1,0:T(8,128)(2,1)S(1)}, bf16[160,2560]{1,0:T(8,128)(2,1)S(1)}, u32[]{:S(2)}, u32[]{:S(2)}) collective-permute-start(bf16[160,2560]{1,0:T(8,128)(2,1)S(1)} %get-tuple-element.89), channel_id=1, source_target_pairs={{0,32},{32,0},{16,48},{48,16},{64,96},{96,64},{80,112},{112,80},{1... | collective-permute-start | bytes 2457608 | tf_op jit(solution)/shard_map/cond/branch_1_fun/ppermute | solution.py:26
